TPU v7x, 32 devices: a whole 2x2x4 slice. The times are simulated.
32 devices in a mesh: group: 2 (over x), row: 8 (over z, y), expert: 2 (over core).
Axes of the slice: x: 2, y: 2, z: 4, core: 2. Of those that a mesh axis runs over, the one named last changes fastest.
Arguments:
- tokens: bfloat16 [2, 128, 128, 1024], P('group', ('row', 'expert')), parts along dimension 0, may hold values from -30 to 30
- ln_first: float32 [1024], replicated, may hold values from 0.5 to 1.5
- spec_first: bfloat16 [2, 8, 128, 128], replicated, may hold values from -0.375 to 0.375
- spec_second: bfloat16 [2, 8, 128, 128], replicated, may hold values from -0.375 to 0.375
- spec_bias: float32 [2, 1024], replicated, may hold values from -3 to 3
- ln_second: float32 [1024], replicated, may hold values from 0.5 to 1.5
- routing: int32 [2, 128, 128, 4], P('group', ('row', 'expert')), parts along dimension 0, may hold values from 0 to 3, as said below
- combine: float32 [2, 128, 128, 4], P('group', ('row', 'expert')), parts along dimension 0, may hold values from 0.1 to 0.6
- up_weight: bfloat16 [8, 1024, 1536], P('row'), may hold values from -0.1875 to 0.1875
- down_weight: bfloat16 [8, 1536, 1024], P('row'), may hold values from -0.109375 to 0.109375
Outputs:
- block_out: bfloat16 [2, 128, 128, 1024], P('group', ('row', 'expert')), parts along dimension 0
There are 2 independent parts, one for each index of `group`. A program takes and returns all parts, laid end to end along the dimension named above; an argument that names none is the same for every part. Nothing has to cross between parts.
Inputs may be any that keep to these rules, and one draw needn't show every extreme that they name: `routing`: each token names 4 different experts, and the 1024 tokens held by each index of row+expert name every expert exactly 1024 times.
All inputs are finite; a program needn't handle non-finite values.
Results may differ from a plain program's by a relative error of at most 0.006.
Values may be sent and summed in bfloat16 or wider, within the bound.
A program may use at most 128 MiB of HBM per device.

v0:
```python
import math

import jax
import jax.numpy as jnp
import numpy as np
from jax import lax
from jax.experimental import pallas as pl
from jax.experimental.pallas import tpu as pltpu
from jax.sharding import PartitionSpec as P


def from_partner(value, axis, stride):
    mask = 2**stride
    pairs = [(source, source ^ mask) for source in range(lax.axis_size(axis))]
    return lax.ppermute(value, axis, pairs)


def twiddle(length):
    counter = jnp.arange(length, dtype=jnp.float32)
    angle = 2.0 * math.pi / length * jnp.mod(jnp.outer(counter, counter), float(length))
    return (jnp.cos(angle), jnp.sin(angle))


def layer_norm(values, gain):
    values = values.astype(jnp.float32)
    center = values - jnp.mean(values, axis=-1, keepdims=True)
    spread = jnp.mean(center * center, axis=-1, keepdims=True)
    return center * lax.rsqrt(spread + 1e-05) * gain


def product(left, right, form):
    return jnp.einsum(form, left, right, preferred_element_type=jnp.float32)


def complex_blocks(real_in, imag_in, weight):
    form = "ghkbi,bio->ghkbo"
    real_out = product(real_in, weight[0], form) - product(imag_in, weight[1], form)
    imag_out = product(real_in, weight[1], form) + product(imag_in, weight[0], form)
    return (real_out, imag_out)


def block_mlp(modes, first, second, bias):
    dims = modes.shape
    nblocks = first.shape[1]
    bwidth = first.shape[2]
    real_part = modes[:, 0].reshape(dims[0], dims[2], dims[3], nblocks, bwidth)
    imag_part = modes[:, 1].reshape(dims[0], dims[2], dims[3], nblocks, bwidth)
    hid_real, hid_imag = complex_blocks(real_part, imag_part, first)
    hid_real = jax.nn.relu(hid_real + bias[0].reshape(nblocks, bwidth)).astype(jnp.bfloat16)
    hid_imag = jax.nn.relu(hid_imag + bias[1].reshape(nblocks, bwidth)).astype(jnp.bfloat16)
    out_real, out_imag = complex_blocks(hid_real, hid_imag, second)
    return jnp.stack([out_real, out_imag], axis=1).reshape(dims).astype(jnp.bfloat16)


def run_expert(arrived, up_full, down_full):
    in_shape = arrived.shape
    width = arrived.shape[2]
    hidden = jax.nn.gelu(
        jnp.dot(arrived.reshape(-1, width), up_full, preferred_element_type=jnp.float32),
        approximate=True,
    ).astype(jnp.bfloat16)
    partial_out = jnp.dot(hidden, down_full, preferred_element_type=jnp.float32).reshape(
        in_shape[0], in_shape[1], width
    )
    return lax.all_to_all(
        partial_out.astype(jnp.bfloat16), "row", split_axis=0, concat_axis=0, tiled=True
    ).astype(partial_out.dtype)


def per_device(
    tokens,
    ln_first,
    spec_first,
    spec_second,
    spec_bias,
    ln_second,
    routing,
    combine,
    up_weight,
    down_weight,
):
    grid_len = tokens.shape[2]
    width = tokens.shape[3]
    cosine, sine = twiddle(grid_len)
    forward_cols = jnp.stack([cosine, -sine], axis=1).astype(jnp.bfloat16)
    forward_rows = jnp.stack(
        [jnp.stack([cosine, sine], axis=1), jnp.stack([-sine, cosine], axis=1)], axis=0
    ).astype(jnp.bfloat16)
    inverse_rows = jnp.stack(
        [jnp.stack([cosine, -sine], axis=1), jnp.stack([sine, cosine], axis=1)], axis=0
    ).astype(jnp.bfloat16)
    inverse_cols = jnp.stack([cosine, -sine], axis=0).astype(jnp.bfloat16)
    normed_first = layer_norm(tokens, ln_first).astype(jnp.bfloat16)
    col_spec = product(normed_first, forward_cols, "ghwd,wck->gchkd").astype(jnp.bfloat16)
    by_column = lax.all_to_all(col_spec, ("row", "expert"), split_axis=3, concat_axis=2, tiled=True)
    modes = (product(forward_rows, by_column, "amch,gchkd->gamkd") * (1.0 / grid_len)).astype(
        jnp.bfloat16
    )
    mixed_modes = block_mlp(modes, spec_first, spec_second, spec_bias)
    row_back = product(inverse_rows, mixed_modes, "amch,gchkd->gamkd").astype(jnp.bfloat16)
    by_row = lax.all_to_all(row_back, ("row", "expert"), split_axis=2, concat_axis=3, tiled=True)
    mixing = product(by_row, inverse_cols, "gchkd,ckw->ghwd") * (1.0 / grid_len)
    residual = (tokens.astype(jnp.float32) + mixing).astype(jnp.bfloat16)
    normed = layer_norm(residual, ln_second).astype(jnp.bfloat16).reshape(-1, width)
    n_tokens = normed.shape[0]
    top_count = routing.shape[-1]
    experts = lax.axis_size("row") // 2
    capacity = n_tokens * top_count // experts
    flat_route = routing.reshape(-1)
    one_hot = (flat_route[:, None] == jnp.arange(experts, dtype=jnp.int32)[None, :]).astype(
        jnp.int32
    )
    earlier = jnp.cumsum(one_hot, axis=0) - one_hot
    slot_index = flat_route * capacity + jnp.sum(earlier * one_hot, axis=1)
    token_of = jnp.arange(n_tokens * top_count, dtype=jnp.int32) // top_count
    source_row = jnp.zeros((experts * capacity,), jnp.int32).at[slot_index].set(token_of)
    send_rows = normed[source_row].reshape(experts, capacity, width)
    partner_up, partner_down = from_partner((up_weight, down_weight), "row", 0)
    up_full = jnp.concatenate([up_weight[0], partner_up[0]], axis=1)
    down_full = jnp.concatenate([down_weight[0], partner_down[0]], axis=0)
    outgoing = send_rows.reshape(experts * 2, capacity // 2, width)
    returned = run_expert(
        lax.all_to_all(outgoing, "row", split_axis=0, concat_axis=0, tiled=True), up_full, down_full
    )
    results = returned.reshape(experts, capacity, width)
    gathered = results.reshape(-1, width)[slot_index].reshape(n_tokens, top_count, width)
    moe_out = jnp.sum(gathered * combine.reshape(n_tokens, top_count, 1), axis=1)
    final = residual.reshape(-1, width).astype(jnp.float32) + moe_out
    return final.reshape(tokens.shape).astype(jnp.bfloat16)


LANES = 256
PARTS = 2


def rank_tables(length, ranks):
    counter = np.arange(length)
    angle = 2.0 * np.pi / length * np.mod(np.outer(counter, counter), length)
    cosine, sine = np.cos(angle), np.sin(angle)
    half = length // 2
    second = -sine[:half]
    second[0] = cosine[half]
    packed = np.stack([cosine[:half], second])
    packed = packed.reshape(2, ranks, half // ranks, length).transpose(1, 0, 2, 3)
    packed = packed.reshape(length, length)
    tables = np.stack([cosine, sine, packed, packed.T])
    return jnp.asarray(tables, jnp.float32).astype(jnp.bfloat16)


def pick(index, values):
    out = values[-1]
    for place, value in enumerate(values[:-1]):
        out = jnp.where(index == place, value, out)
    return out


def norm_rows(values, gain):
    center = values - jnp.mean(values, axis=-1, keepdims=True)
    spread = jnp.mean(center * center, axis=-1, keepdims=True)
    return center * lax.rsqrt(spread + 1e-05) * gain


def block_kernel(
    sizes,
    tokens_ref,
    ln_first_ref,
    ln_second_ref,
    tables_ref,
    first_ref,
    second_ref,
    bias_ref,
    gates_ref,
    up_hbm,
    down_hbm,
    out_ref,
    columns,
    columns_t,
    rows_d,
    rows_dt,
    spec_send,
    spec_recv,
    back_send,
    back_recv,
    resid,
    acts,
    gates,
    total,
    ups,
    downs,
    a2a_send,
    a2a_recv,
    z_send,
    z_recv,
    x_send,
    x_recv,
    c_send,
    c_recv,
    swap_send,
    swap_recv,
    local_sem,
):
    groups, rows_axis, cores = sizes
    planes = rows_axis // 2
    ranks = rows_axis * cores
    group, row, core = lax.axis_index("group"), lax.axis_index("row"), lax.axis_index("expert")
    plane = row // 2
    me = row * cores + core
    n_tokens, width = tokens_ref.shape
    lanes = spec_send.shape[2]
    chunks = width // lanes
    grid_len = tables_ref.shape[1]
    slots = grid_len // 2 // ranks
    block_rows = n_tokens // ranks
    bwidth = first_ref.shape[2]
    per_step = lanes // bwidth
    scale = 1.0 / grid_len
    hidden = ups.shape[2]
    step = n_tokens // 2
    bf16 = jnp.bfloat16

    def device(g, r, c):
        return {"group": g, "row": r, "expert": c}

    def remote(source, target, send, recv, where):
        return pltpu.make_async_remote_copy(
            src_ref=source,
            dst_ref=target,
            send_sem=send,
            recv_sem=recv,
            device_id=where,
            device_id_type=pl.DeviceIdType.MESH,
        )

    barrier = pltpu.get_barrier_semaphore()
    for offset in range(1, ranks):
        other = lax.rem(me + offset, ranks)
        pl.semaphore_signal(
            barrier,
            inc=1,
            device_id=device(group, other // cores, other % cores),
            device_id_type=pl.DeviceIdType.MESH,
        )
    pl.semaphore_signal(
        barrier,
        inc=1,
        device_id=device(1 - group, row, core),
        device_id_type=pl.DeviceIdType.MESH,
    )
    pl.semaphore_wait(barrier, ranks)

    shares = groups * cores
    share = group * cores + core
    side_share = (1 - group) * cores + core
    pieces = 2 * PARTS

    def view(ref, base, quarter, piece):
        size = ref.shape[1] // shares // PARTS
        start = (quarter * PARTS + piece % PARTS) * size
        return ref.at[base, pl.ds(pl.multiple_of(start, 32), size), :]

    def held(expert, quarter, piece):
        return view(ups if piece < PARTS else downs, expert, quarter, piece)

    def source(piece):
        return view(up_hbm if piece < PARTS else down_hbm, 0, share, piece)

    def plane_copy(expert, piece, src, way, target_plane):
        return remote(
            src,
            held(expert, share, piece),
            z_send.at[way, expert, piece],
            z_recv.at[expert, piece],
            device(group, 2 * target_plane + row % 2, core),
        )

    def side_copy(expert, piece):
        return remote(
            held(expert, share, piece),
            held(expert, share, piece),
            x_send.at[expert, piece],
            x_recv.at[expert, piece],
            device(1 - group, row, core),
        )

    def core_copy(expert, piece, which):
        part = held(expert, side_share if which else share, piece)
        return remote(
            part,
            part,
            c_send.at[which, expert, piece],
            c_recv.at[which, expert, piece],
            device(group, row, 1 - core),
        )

    near = plane + 1 - 2 * (plane % 2)
    far = plane - 1 + 2 * (plane % 2)
    inner = (far >= 0) & (far < planes)
    safe_far = jnp.clip(far, 0, planes - 1)
    arrivals = [[2 * (p // 2) + 1 - p % 2] for p in range(planes)]
    for p in range(planes):
        arrivals[p] += sorted((q for q in range(planes) if q // 2 != p // 2), key=lambda q: abs(q - p))
    expert_at = [plane] + [pick(plane, [a[t] for a in arrivals]) for t in range(planes - 1)]

    def own_copies(piece):
        return plane_copy(plane, piece, source(piece), 0, near)

    def far_own(piece):
        return plane_copy(plane, piece, source(piece), 1, safe_far)

    def forward(t, piece):
        expert = expert_at[t]
        target = safe_far if t == 1 else near
        return plane_copy(expert, piece, held(expert, share, piece), 0, target)

    def relay(t, piece, stage):
        expert = expert_at[t]
        if stage == 0:
            plane_copy(expert, piece, held(expert, share, piece), 0, near).wait_recv()
            if t > 1:

                @pl.when(inner)
                def _():
                    forward(t, piece).start()

            side_copy(expert, piece).start()
            core_copy(expert, piece, 0).start()
        else:
            side_copy(expert, piece).wait_recv()
            core_copy(expert, piece, 1).start()

    def ready(t):
        for piece in range(pieces):
            for which in range(2):
                core_copy(expert_at[t], piece, which).wait_recv()

    half = row % 2
    partner = device(group, row + 1 - 2 * half, core)
    gate_copy = remote(gates_ref, gates.at[1], swap_send.at[0], swap_recv.at[0], partner)
    gate_copy.start()
    for piece in range(PARTS):
        own_copies(piece).start()
    up_local = pltpu.make_async_copy(up_hbm.at[0], ups.at[plane], local_sem.at[0])
    down_local = pltpu.make_async_copy(down_hbm.at[0], downs.at[plane], local_sem.at[1])
    up_local.start()
    down_local.start()

    @pl.loop(0, n_tokens // grid_len)
    def _(index):
        rows = pl.ds(pl.multiple_of(index * grid_len, grid_len), grid_len)
        acts[0, rows, :] = norm_rows(tokens_ref[rows, :].astype(jnp.float32), ln_first_ref[...]).astype(
            bf16
        )

    my_rows = n_tokens // grid_len
    spread = jnp.broadcast_to(
        tables_ref[2].astype(jnp.float32)[:, None, :], (grid_len, my_rows, grid_len)
    ).reshape(n_tokens, grid_len)
    place = lax.broadcasted_iota(jnp.int32, (n_tokens, grid_len), 0) % my_rows
    for index in range(my_rows):
        columns[:, index * grid_len : (index + 1) * grid_len] = jnp.where(
            place == index, spread, 0.0
        ).astype(bf16)

    order = sorted(range(1, ranks), key=lambda offset: abs(offset - ranks // 2))

    def exchange(stage, send_ref, recv_ref, chunk, offset):
        other = lax.rem(me + offset, ranks)
        return remote(
            send_ref.at[chunk, pl.ds(pl.multiple_of(other * block_rows, block_rows), block_rows), :],
            recv_ref.at[chunk, pl.ds(pl.multiple_of(me * block_rows, block_rows), block_rows), :],
            a2a_send.at[stage, chunk, offset],
            a2a_recv.at[stage, chunk, offset],
            device(group, other // cores, other % cores),
        )

    def arrived(stage, send_ref, recv_ref, chunk, offset):
        other = lax.rem(me + ranks - offset, ranks)
        return remote(
            send_ref.at[chunk, pl.ds(pl.multiple_of(me * block_rows, block_rows), block_rows), :],
            recv_ref.at[chunk, pl.ds(pl.multiple_of(other * block_rows, block_rows), block_rows), :],
            a2a_send.at[stage, chunk, offset],
            a2a_recv.at[stage, chunk, offset],
            device(group, other // cores, other % cores),
        )

    def keep_own(send_ref, recv_ref, chunk):
        mine = pl.ds(pl.multiple_of(me * block_rows, block_rows), block_rows)
        recv_ref[chunk, mine, :] = send_ref[chunk, mine, :]

    @pl.loop(0, chunks)
    def _(chunk):
        cut = pl.ds(pl.multiple_of(chunk * lanes, lanes), lanes)
        spec_send[chunk] = jnp.dot(
            columns[...], acts[0, :, cut], preferred_element_type=jnp.float32
        ).astype(bf16)
        for offset in order:
            exchange(0, spec_send, spec_recv, chunk, offset).start()
        keep_own(spec_send, spec_recv, chunk)

    picker = lax.broadcasted_iota(jnp.int32, (grid_len, n_tokens), 1) // my_rows
    picker = picker == lax.broadcasted_iota(jnp.int32, (grid_len, n_tokens), 0)
    picker = jnp.where(picker, 1.0, 0.0).astype(bf16)
    spread_t = jnp.dot(tables_ref[3], picker, preferred_element_type=jnp.float32)
    place_t = lax.broadcasted_iota(jnp.int32, (grid_len, n_tokens), 1) % my_rows
    for index in range(my_rows):
        columns_t[index * grid_len : (index + 1) * grid_len, :] = jnp.where(
            place_t == index, spread_t, 0.0
        ).astype(bf16)
    cosine, sine = tables_ref[0], tables_ref[1]
    none = jnp.zeros_like(cosine)

    def fill(slot, grid):
        for index, (left, right) in enumerate(grid):
            cut = slice(index * grid_len, (index + 1) * grid_len)
            rows_d[slot, cut, :grid_len] = left
            rows_d[slot, cut, grid_len:] = right
            rows_dt[slot, :grid_len, cut] = left
            rows_dt[slot, grid_len:, cut] = right

    usual = [(cosine, sine), (cosine, -sine), (-sine, cosine), (-sine, -cosine)]
    fill(0, usual)

    @pl.when(me == 0)
    def _():
        fill(1, [(cosine, none), (none, cosine), (-sine, none), (none, -sine)])

    @pl.when(me != 0)
    def _():
        fill(1, usual)

    gates[0] = gates_ref[...]
    total[...] = jnp.zeros_like(total)

    def square(ref, block):
        real, imag = ref[0, block], ref[1, block]
        top = jnp.concatenate([real, imag], axis=1)
        return jnp.concatenate([top, jnp.concatenate([-imag, real], axis=1)], axis=0)

    def mix(chunk):
        values = spec_recv[chunk].astype(jnp.float32).reshape(ranks, 2 * slots, my_rows, lanes)
        real_parts, imag_parts = [], []
        for slot in range(slots):
            pair = jnp.concatenate(
                [
                    values[:, slot].reshape(grid_len, lanes),
                    values[:, slots + slot].reshape(grid_len, lanes),
                ],
                axis=0,
            ).astype(bf16)
            matrix = rows_d[1 if slot == 0 else 0]
            modes = jnp.dot(matrix, pair, preferred_element_type=jnp.float32) * scale
            modes = modes.astype(bf16)
            real_parts.append(modes[: 2 * grid_len])
            imag_parts.append(modes[2 * grid_len :])
        real = jnp.concatenate(real_parts, axis=0)
        imag = jnp.concatenate(imag_parts, axis=0)
        mixed_real, mixed_imag = [], []
        for index in range(per_step):
            block = chunk * per_step + index
            cut = slice(index * bwidth, (index + 1) * bwidth)
            both = jnp.concatenate([real[:, cut], imag[:, cut]], axis=1)
            place = pl.ds(pl.multiple_of(block * bwidth, bwidth), bwidth)
            bias = jnp.concatenate([bias_ref[0:1, place], bias_ref[1:2, place]], axis=1)
            hid = jnp.dot(both, square(first_ref, block), preferred_element_type=jnp.float32) + bias
            hid = jnp.maximum(hid, 0.0).astype(bf16)
            mixed = jnp.dot(hid, square(second_ref, block), preferred_element_type=jnp.float32)
            mixed = mixed.astype(bf16)
            mixed_real.append(mixed[:, :bwidth])
            mixed_imag.append(mixed[:, bwidth:])
        real = jnp.concatenate(mixed_real, axis=1)
        imag = jnp.concatenate(mixed_imag, axis=1)
        back_real, back_imag = [], []
        for slot in range(slots):
            cut = slice(slot * 2 * grid_len, (slot + 1) * 2 * grid_len)
            column = jnp.concatenate([real[cut], imag[cut]], axis=0)
            matrix = rows_dt[1 if slot == 0 else 0]
            back = jnp.dot(matrix, column, preferred_element_type=jnp.float32)
            back_real.append(back[:grid_len].reshape(ranks, my_rows, lanes))
            back_imag.append(back[grid_len:].reshape(ranks, my_rows, lanes))
        out = jnp.stack(back_real + back_imag, axis=1).reshape(n_tokens, lanes)
        back_send[chunk] = out.astype(bf16)

    @pl.loop(0, chunks)
    def _(chunk):
        @pl.when(chunk == 1)
        def _():
            for piece in range(PARTS):
                relay(1, piece, 0)

        @pl.when(chunk == 2)
        def _():
            for piece in range(PARTS):
                relay(1, piece, 1)

        for offset in order:
            arrived(0, spec_send, spec_recv, chunk, offset).wait_recv()
        mix(chunk)
        for offset in order:
            exchange(1, back_send, back_recv, chunk, offset).start()
        keep_own(back_send, back_recv, chunk)

        @pl.when(chunk == 0)
        def _():
            for piece in range(PARTS, pieces):
                own_copies(piece).start()

    @pl.when(inner)
    def _():
        for piece in range(pieces):
            far_own(piece).start()
        for piece in range(PARTS):
            forward(1, piece).start()

    @pl.loop(0, chunks)
    def _(chunk):
        @pl.when(chunk == 2)
        def _():
            for piece in range(PARTS, pieces):
                relay(1, piece, 0)

            @pl.when(inner)
            def _():
                for piece in range(PARTS, pieces):
                    forward(1, piece).start()

        for offset in order:
            arrived(1, back_send, back_recv, chunk, offset).wait_recv()
        cut = pl.ds(pl.multiple_of(chunk * lanes, lanes), lanes)
        mixing = jnp.dot(columns_t[...], back_recv[chunk], preferred_element_type=jnp.float32) * scale
        resid[:, cut] = (tokens_ref[:, cut].astype(jnp.float32) + mixing).astype(bf16)

    def swap_copy(block):
        rows = pl.ds(block * step, step)
        return remote(
            acts.at[0, rows, :],
            acts.at[1, rows, :],
            swap_send.at[1 + block],
            swap_recv.at[1 + block],
            partner,
        )

    def return_copy(block):
        rows = pl.ds(pl.multiple_of(block * step, step), step)
        return remote(
            spec_send.at[:, rows, :],
            spec_recv.at[:, rows, :],
            swap_send.at[3 + block],
            swap_recv.at[3 + block],
            partner,
        )

    for block in range(2):

        @pl.loop(0, my_rows // 2)
        def _(index):
            start = block * step + index * grid_len
            rows = pl.ds(pl.multiple_of(start, grid_len), grid_len)
            acts[0, rows, :] = norm_rows(
                resid[rows, :].astype(jnp.float32), ln_second_ref[...]
            ).astype(bf16)

        swap_copy(block).start()

    @pl.loop(0, chunks)
    def _(chunk):
        for offset in order:
            exchange(0, spec_send, spec_recv, chunk, offset).wait_send()

    plan = [(0, 0, 0), (0, 1, 0), (0, 0, 1), (0, 1, 1)]
    plan += [(1, 0, 0), (1, 0, 1), (1, 1, 0), (1, 1, 1)]
    plan += [(1, 0, 2), (1, 1, 2), (0, 0, 2), (0, 1, 2)]
    plan += [(1, 0, 3), (1, 1, 3), (0, 0, 3), (0, 1, 3)]
    relays = {}

    def at(place_inner, place_outer, t, piece, stage):
        relays[(t, piece, stage)] = jnp.where(inner, place_inner, place_outer)

    for piece in range(pieces):
        share_of = (piece * 4) // pieces
        at((2, 4, 5, 7)[share_of], (4, 5, 7, 8)[share_of], 2, piece, 0)
        at((4, 6, 7, 8)[share_of], (6, 7, 8, 8)[share_of], 2, piece, 1)
        at((8, 9, 11, 12)[share_of], (9, 11, 12, 12)[share_of], 3, piece, 0)
        at((10, 11, 12, 12)[share_of], (11, 12, 12, 12)[share_of], 3, piece, 1)

    def lift(who, rows, expert, cut):
        return jnp.dot(
            acts[who, rows, :], ups[expert, :, cut], preferred_element_type=jnp.float32
        )

    @pl.loop(0, len(plan))
    def _(item):
        who = pick(item, [p[0] for p in plan])
        block = pick(item, [p[1] for p in plan])
        turn = pick(item, [p[2] for p in plan])

        @pl.when(item == 0)
        def _():
            up_local.wait()
            down_local.wait()
            for piece in range(PARTS, pieces):
                relay(1, piece, 1)

        for (t, piece, stage), place in sorted(relays.items(), key=lambda r: (r[0][0], r[0][2], r[0][1])):

            @pl.when(item == place)
            def _():
                relay(t, piece, stage)

        for t, place in ((1, 2), (2, 8), (3, 12)):

            @pl.when(item == place)
            def _():
                ready(t)

        for index, place in ((0, 4), (1, 6)):

            @pl.when(item == place)
            def _():
                swap_copy(index).wait_recv()

        @pl.when(item == 4)
        def _():
            gate_copy.wait_recv()

        expert = pick(turn, expert_at)
        rows = pl.ds(pl.multiple_of(block * step, step), step)
        wide = 512 if hidden % 512 == 0 else hidden
        cuts = [pl.ds(start, wide) for start in range(0, hidden, wide)]
        out, ahead = None, lift(who, rows, expert, cuts[0])
        for index, cut in enumerate(cuts):
            raw = ahead
            if index + 1 < len(cuts):
                ahead = lift(who, rows, expert, cuts[index + 1])
            active = jax.nn.gelu(raw, approximate=True).astype(bf16)
            part = jnp.dot(active, downs[expert, cut, :], preferred_element_type=jnp.float32)
            out = part if out is None else out + part
        lane = lax.broadcasted_iota(jnp.int32, (step, gates.shape[2]), 1)
        gate = jnp.sum(jnp.where(lane == expert, gates[who, rows, :], 0.0), axis=1, keepdims=True)
        total[who, rows, :] = total[who, rows, :] + gate * out

        @pl.when((who == 1) & (turn == planes - 1))
        def _():
            for chunk in range(chunks):
                cut = slice(chunk * lanes, (chunk + 1) * lanes)
                spec_send[chunk, rows, :] = total[1, rows, cut].astype(bf16)
            return_copy(block).start()

    for block in range(2):
        return_copy(block).wait_recv()
        rows = pl.ds(block * step, step)
        for chunk in range(chunks):
            cut = slice(chunk * lanes, (chunk + 1) * lanes)
            final = resid[rows, cut].astype(jnp.float32) + total[0, rows, cut]
            final = final + spec_recv[chunk, rows, :].astype(jnp.float32)
            out_ref[rows, cut] = final.astype(bf16)

    for block in range(2):
        swap_copy(block).wait_send()
        return_copy(block).wait_send()
    gate_copy.wait_send()

    @pl.loop(0, chunks)
    def _(chunk):
        for offset in order:
            exchange(1, back_send, back_recv, chunk, offset).wait_send()

    for piece in range(pieces):
        own_copies(piece).wait_send()
        for t in range(1, planes):
            side_copy(expert_at[t], piece).wait_send()
            for which in range(2):
                core_copy(expert_at[t], piece, which).wait_send()

    @pl.when(inner)
    def _():
        for piece in range(pieces):
            far_own(piece).wait_send()
            for t in range(1, planes):
                forward(t, piece).wait_send()


def per_device_fused(
    sizes,
    tokens,
    ln_first,
    spec_first,
    spec_second,
    spec_bias,
    ln_second,
    routing,
    combine,
    up_weight,
    down_weight,
):
    groups, rows_axis, cores = sizes
    ranks, planes = rows_axis * cores, rows_axis // 2
    _, my_rows, grid_len, width = tokens.shape
    n_tokens = my_rows * grid_len
    lanes = LANES
    chunks = width // lanes
    route = routing.reshape(n_tokens, -1)
    weight = combine.reshape(n_tokens, -1)
    spot = jnp.arange(128, dtype=jnp.int32)
    gates = jnp.zeros((n_tokens, 128), jnp.float32)
    for k in range(route.shape[1]):
        gates = gates + jnp.where(route[:, k : k + 1] == spot[None, :], weight[:, k : k + 1], 0.0)
    hidden = up_weight.shape[2]
    bf16 = jnp.bfloat16
    pieces = 2 * PARTS
    vmem = pl.BlockSpec(memory_space=pltpu.VMEM)
    hbm = pl.BlockSpec(memory_space=pl.ANY)
    dma = pltpu.SemaphoreType.DMA
    out = pl.pallas_call(
        lambda *refs: block_kernel(sizes, *refs),
        in_specs=[vmem] * 8 + [hbm] * 2,
        out_specs=vmem,
        out_shape=jax.ShapeDtypeStruct((n_tokens, width), bf16),
        scratch_shapes=[
            pltpu.VMEM((n_tokens, n_tokens), bf16),
            pltpu.VMEM((n_tokens, n_tokens), bf16),
            pltpu.VMEM((2, 4 * grid_len, 2 * grid_len), bf16),
            pltpu.VMEM((2, 2 * grid_len, 4 * grid_len), bf16),
            pltpu.VMEM((chunks, n_tokens, lanes), bf16),
            pltpu.VMEM((chunks, n_tokens, lanes), bf16),
            pltpu.VMEM((chunks, n_tokens, lanes), bf16),
            pltpu.VMEM((chunks, n_tokens, lanes), bf16),
            pltpu.VMEM((n_tokens, width), bf16),
            pltpu.VMEM((2, n_tokens, width), bf16),
            pltpu.VMEM((2, n_tokens, 128), jnp.float32),
            pltpu.VMEM((2, n_tokens, width), jnp.float32),
            pltpu.VMEM((planes,) + up_weight.shape[1:], bf16),
            pltpu.VMEM((planes,) + down_weight.shape[1:], bf16),
            dma((2, chunks, ranks)),
            dma((2, chunks, ranks)),
            dma((2, planes, pieces)),
            dma((planes, pieces)),
            dma((planes, pieces)),
            dma((planes, pieces)),
            dma((2, planes, pieces)),
            dma((2, planes, pieces)),
            dma((5,)),
            dma((5,)),
            dma((2,)),
        ],
        compiler_params=pltpu.CompilerParams(
            collective_id=0, has_side_effects=True, vmem_limit_bytes=67043328
        ),
        name="block",
    )(
        tokens.reshape(n_tokens, width),
        ln_first.reshape(1, width),
        ln_second.reshape(1, width),
        rank_tables(grid_len, ranks),
        spec_first,
        spec_second,
        spec_bias,
        gates,
        up_weight,
        down_weight,
    )
    return out.reshape(tokens.shape)


def solution(mesh):
    shape = mesh.shape
    group, row, expert = shape["group"], shape["row"], shape["expert"]
    cells = P("group", ("row", "expert"), None, None)
    weights = P("row", None, None)
    ins = (cells, P(), P(), P(), P(), P(), cells, cells, weights, weights)

    def run(*args):
        tokens, first, routing = args[0], args[2], args[6]
        ranks, planes = row * expert, row // 2
        fused = group == 2 and expert == 2 and planes == 4 and routing.shape[-1] == planes
        fused = fused and tokens.shape[0] == group and tokens.shape[1] == 8 * ranks
        fused = fused and (tokens.shape[2] // 2) % ranks == 0 and tokens.shape[2] == 128
        fused = fused and tokens.shape[3] % LANES == 0 and LANES % first.shape[2] == 0
        fused = fused and args[8].shape[1] % 256 == 0 and args[9].shape[1] % 256 == 0
        if fused:
            body = lambda *blocks: per_device_fused((group, row, expert), *blocks)
        else:
            body = per_device
        call = jax.shard_map(body, mesh=mesh, in_specs=ins, out_specs=cells, check_vma=False)
        return call(*args)

    return run
```

profile of v0, /device:TPU:1, one launch (start us, length us, event | category | flops | bytes accessed | tf_op | source)
XLA Modules:
  0.0 283.1 jit_solution(17100669808057872344)
XLA Ops:
  0.0 0.9 fusion
  0.9 0.9 fusion.1
  1.8 2.4 select_add_fusion.refs_7_
  4.1 275.9 %block.1 = bf16[1024,1024]{1,0:T(8,128)(2,1)} custom-call(bf16[1024,1024]{1,0:T(8,128)(2,1)} %bitcast.15, f32[1,1024]{1,0:T(1,128)} %bitcast.26, f32[1,1024]{1,0:T(1,128)} %bitcast.27, bf16[4,128,128]{2,1,0:T(8,128)(2,1)} %constant.10.refs_3_, bf16[2,8,128,128]{3,2,1,0:T(8,128)(2,1)} %refs_4_.1, bf16[2,8,128,128]{3,2,1,0:T(8,128)(2,1)} %refs_5_.1, ...), custom_call_target="tpu_custom_call" | custom-call | tf_op jit(solution)/shard_map/block/pallas_call | solution.py:713
  280.1 3.1 %copy.15 = bf16[1,8,128,1024]{3,2,1,0:T(8,128)(2,1)} copy(bf16[1,8,128,1024]{3,2,1,0:T(8,128)(2,1)} %bitcast.14) | data formatting | bytes 4194304
where the time goes:
time: 285 us; the launch traced here: 283 us
  Pallas kernels  276 us (97%)
  local copies, waits for them, and re-layouts  4.85 us (2%)
    pallas_call x1, Pallas kernels, per_device_fused(): pl.pallas_call(lambda *refs: block_kernel(sizes, *refs), in_specs=[vmem]...  276 us

commit v1 on v0

--- a/solution.py
+++ b/solution.py
@@ -130,7 +130,8 @@
 
 
 LANES = 256
-PARTS = 2
+PARTS = 4
+EARLY_CHUNK = 3
 
 
 def rank_tables(length, ranks):
@@ -169,12 +170,12 @@
     first_ref,
     second_ref,
     bias_ref,
-    gates_ref,
+    route_ref,
+    weight_ref,
     up_hbm,
     down_hbm,
     out_ref,
     columns,
-    columns_t,
     rows_d,
     rows_dt,
     spec_send,
@@ -246,6 +247,14 @@
         device_id=device(1 - group, row, core),
         device_id_type=pl.DeviceIdType.MESH,
     )
+
+    @pl.loop(0, n_tokens // grid_len)
+    def _(index):
+        rows = pl.ds(pl.multiple_of(index * grid_len, grid_len), grid_len)
+        acts[0, rows, :] = norm_rows(tokens_ref[rows, :].astype(jnp.float32), ln_first_ref[...]).astype(
+            bf16
+        )
+
     pl.semaphore_wait(barrier, ranks)
 
     shares = groups * cores
@@ -335,21 +344,21 @@
 
     half = row % 2
     partner = device(group, row + 1 - 2 * half, core)
-    gate_copy = remote(gates_ref, gates.at[1], swap_send.at[0], swap_recv.at[0], partner)
-    gate_copy.start()
+    gate_copy = remote(gates.at[0], gates.at[1], swap_send.at[0], swap_recv.at[0], partner)
     for piece in range(PARTS):
         own_copies(piece).start()
+
+    early = pieces // 2
+
+    @pl.when(inner)
+    def _():
+        for piece in range(early // 2):
+            far_own(piece).start()
+
     up_local = pltpu.make_async_copy(up_hbm.at[0], ups.at[plane], local_sem.at[0])
     down_local = pltpu.make_async_copy(down_hbm.at[0], downs.at[plane], local_sem.at[1])
     up_local.start()
     down_local.start()
-
-    @pl.loop(0, n_tokens // grid_len)
-    def _(index):
-        rows = pl.ds(pl.multiple_of(index * grid_len, grid_len), grid_len)
-        acts[0, rows, :] = norm_rows(tokens_ref[rows, :].astype(jnp.float32), ln_first_ref[...]).astype(
-            bf16
-        )
 
     my_rows = n_tokens // grid_len
     spread = jnp.broadcast_to(
@@ -403,7 +412,7 @@
     spread_t = jnp.dot(tables_ref[3], picker, preferred_element_type=jnp.float32)
     place_t = lax.broadcasted_iota(jnp.int32, (grid_len, n_tokens), 1) % my_rows
     for index in range(my_rows):
-        columns_t[index * grid_len : (index + 1) * grid_len, :] = jnp.where(
+        columns[index * grid_len : (index + 1) * grid_len, :] = jnp.where(
             place_t == index, spread_t, 0.0
         ).astype(bf16)
     cosine, sine = tables_ref[0], tables_ref[1]
@@ -428,7 +437,12 @@
     def _():
         fill(1, usual)
 
-    gates[0] = gates_ref[...]
+    lane = lax.broadcasted_iota(jnp.int32, gates.shape[1:], 1)
+    chosen = jnp.zeros(gates.shape[1:], jnp.float32)
+    for k in range(route_ref.shape[1]):
+        hit = route_ref[:, k : k + 1] == lane
+        chosen = chosen + jnp.where(hit, weight_ref[:, k : k + 1], 0.0)
+    gates[0] = chosen
     total[...] = jnp.zeros_like(total)
 
     def square(ref, block):
@@ -482,15 +496,10 @@
 
     @pl.loop(0, chunks)
     def _(chunk):
-        @pl.when(chunk == 1)
+        @pl.when((chunk == EARLY_CHUNK) & inner)
         def _():
-            for piece in range(PARTS):
-                relay(1, piece, 0)
-
-        @pl.when(chunk == 2)
-        def _():
-            for piece in range(PARTS):
-                relay(1, piece, 1)
+            for piece in range(early // 2):
+                relay(2, piece, 0)
 
         for offset in order:
             arrived(0, spec_send, spec_recv, chunk, offset).wait_recv()
@@ -503,10 +512,19 @@
         def _():
             for piece in range(PARTS, pieces):
                 own_copies(piece).start()
+            gate_copy.start()
+
+        @pl.when((chunk == 1) & inner)
+        def _():
+            for piece in range(early // 2, early):
+                far_own(piece).start()
+
+    for piece in range(PARTS):
+        relay(1, piece, 0)
 
     @pl.when(inner)
     def _():
-        for piece in range(pieces):
+        for piece in range(early, pieces):
             far_own(piece).start()
         for piece in range(PARTS):
             forward(1, piece).start()
@@ -515,6 +533,8 @@
     def _(chunk):
         @pl.when(chunk == 2)
         def _():
+            for piece in range(PARTS):
+                relay(1, piece, 1)
             for piece in range(PARTS, pieces):
                 relay(1, piece, 0)
 
@@ -522,11 +542,13 @@
             def _():
                 for piece in range(PARTS, pieces):
                     forward(1, piece).start()
+                for piece in range(early // 2, early):
+                    relay(2, piece, 0)
 
         for offset in order:
             arrived(1, back_send, back_recv, chunk, offset).wait_recv()
         cut = pl.ds(pl.multiple_of(chunk * lanes, lanes), lanes)
-        mixing = jnp.dot(columns_t[...], back_recv[chunk], preferred_element_type=jnp.float32) * scale
+        mixing = jnp.dot(columns[...], back_recv[chunk], preferred_element_type=jnp.float32) * scale
         resid[:, cut] = (tokens_ref[:, cut].astype(jnp.float32) + mixing).astype(bf16)
 
     def swap_copy(block):
@@ -567,20 +589,35 @@
             exchange(0, spec_send, spec_recv, chunk, offset).wait_send()
 
     plan = [(0, 0, 0), (0, 1, 0), (0, 0, 1), (0, 1, 1)]
-    plan += [(1, 0, 0), (1, 0, 1), (1, 1, 0), (1, 1, 1)]
-    plan += [(1, 0, 2), (1, 1, 2), (0, 0, 2), (0, 1, 2)]
+    plan += [(1, 0, 0), (1, 0, 1), (0, 0, 2), (0, 1, 2)]
+    plan += [(1, 0, 2), (1, 1, 0), (1, 1, 1), (1, 1, 2)]
     plan += [(1, 0, 3), (1, 1, 3), (0, 0, 3), (0, 1, 3)]
-    relays = {}
-
-    def at(place_inner, place_outer, t, piece, stage):
-        relays[(t, piece, stage)] = jnp.where(inner, place_inner, place_outer)
-
-    for piece in range(pieces):
-        share_of = (piece * 4) // pieces
-        at((2, 4, 5, 7)[share_of], (4, 5, 7, 8)[share_of], 2, piece, 0)
-        at((4, 6, 7, 8)[share_of], (6, 7, 8, 8)[share_of], 2, piece, 1)
-        at((8, 9, 11, 12)[share_of], (9, 11, 12, 12)[share_of], 3, piece, 0)
-        at((10, 11, 12, 12)[share_of], (11, 12, 12, 12)[share_of], 3, piece, 1)
+    first_use = [plan.index((0, 0, t)) for t in range(3)] + [12]
+    pace = 35.0 / pieces
+    starts = {
+        True: [0, 4, 9, 14, 24, 29, 34, 38, 43, 48, 52, 57, 61],
+        False: [0, 5, 9, 14, 23, 28, 39, 44, 48, 53, 58, 62, 74],
+    }
+
+    def expected(t, piece, stage, inside):
+        if inside:
+            when = pace * (piece + 1 - early) if t == 2 else pace * (piece + 1 + early)
+            return when + stage * (pace + 1.5)
+        if stage == 0:
+            return pace * piece + (-3 if t == 2 else 32)
+        return pace * piece + (8 if t == 2 else 43)
+
+    def schedule(inside):
+        places = {}
+        for t in (2, 3):
+            for piece in range(pieces):
+                for stage in range(2):
+                    if inside and t == 2 and stage == 0 and piece < early:
+                        continue
+                    when = expected(t, piece, stage, inside)
+                    place = next((k for k, start in enumerate(starts[inside]) if start >= when - 2), 12)
+                    places.setdefault(min(place, first_use[t]), []).append((when, t, piece, stage))
+        return places
 
     def lift(who, rows, expert, cut):
         return jnp.dot(
@@ -597,22 +634,30 @@
         def _():
             up_local.wait()
             down_local.wait()
+
+        @pl.when(item == first_use[1])
+        def _():
             for piece in range(PARTS, pieces):
                 relay(1, piece, 1)
 
-        for (t, piece, stage), place in sorted(relays.items(), key=lambda r: (r[0][0], r[0][2], r[0][1])):
-
-            @pl.when(item == place)
+        for inside in (True, False):
+
+            @pl.when(inner if inside else jnp.logical_not(inner))
             def _():
-                relay(t, piece, stage)
-
-        for t, place in ((1, 2), (2, 8), (3, 12)):
-
-            @pl.when(item == place)
+                for place, passes in sorted(schedule(inside).items()):
+
+                    @pl.when(item == place)
+                    def _():
+                        for _, t, piece, stage in sorted(passes):
+                            relay(t, piece, stage)
+
+        for t in range(1, planes):
+
+            @pl.when(item == first_use[t])
             def _():
                 ready(t)
 
-        for index, place in ((0, 4), (1, 6)):
+        for index, place in ((0, 4), (1, 9)):
 
             @pl.when(item == place)
             def _():
@@ -700,10 +745,6 @@
     chunks = width // lanes
     route = routing.reshape(n_tokens, -1)
     weight = combine.reshape(n_tokens, -1)
-    spot = jnp.arange(128, dtype=jnp.int32)
-    gates = jnp.zeros((n_tokens, 128), jnp.float32)
-    for k in range(route.shape[1]):
-        gates = gates + jnp.where(route[:, k : k + 1] == spot[None, :], weight[:, k : k + 1], 0.0)
     hidden = up_weight.shape[2]
     bf16 = jnp.bfloat16
     pieces = 2 * PARTS
@@ -712,11 +753,10 @@
     dma = pltpu.SemaphoreType.DMA
     out = pl.pallas_call(
         lambda *refs: block_kernel(sizes, *refs),
-        in_specs=[vmem] * 8 + [hbm] * 2,
+        in_specs=[vmem] * 9 + [hbm] * 2,
         out_specs=vmem,
         out_shape=jax.ShapeDtypeStruct((n_tokens, width), bf16),
         scratch_shapes=[
-            pltpu.VMEM((n_tokens, n_tokens), bf16),
             pltpu.VMEM((n_tokens, n_tokens), bf16),
             pltpu.VMEM((2, 4 * grid_len, 2 * grid_len), bf16),
             pltpu.VMEM((2, 2 * grid_len, 4 * grid_len), bf16),
@@ -754,7 +794,8 @@
         spec_first,
         spec_second,
         spec_bias,
-        gates,
+        route,
+        weight,
         up_weight,
         down_weight,
     )

time: 285 us -> 259 us (0.909)
  Pallas kernels: 276 us -> 251 us
    pallas_call x1, Pallas kernels: 276 us -> 251 us  [per_device_fused(): pl.pallas_call(lambda *refs: block_kernel(sizes, *refs), in_specs=[vmem]...]
    unnamed x1 -> x3, local copies, waits for them, and re-layouts: 3.08 us -> 6.56 us
where the time goes in v1:
time: 259 us; the launch traced here: 258 us
  Pallas kernels  251 us (97%)
  local copies, waits for them, and re-layouts  6.56 us (3%)
    pallas_call x1, Pallas kernels, per_device_fused(): pl.pallas_call(lambda *refs: block_kernel(sizes, *refs), in_specs=[vmem]...  251 us
    unnamed x3, local copies, waits for them, and re-layouts  6.56 us

profile of v1, /device:TPU:1, one launch (start us, length us, event | category | flops | bytes accessed | tf_op | source)
XLA Modules:
  0.0 257.8 jit_solution(15568003926400806409)
XLA Ops:
  0.0 1.7 copy.12
  1.7 1.7 copy.13
  3.5 251.3 %block.1 = bf16[1024,1024]{1,0:T(8,128)(2,1)} custom-call(bf16[1024,1024]{1,0:T(8,128)(2,1)} %bitcast.7, f32[1,1024]{1,0:T(1,128)} %bitcast.10, f32[1,1024]{1,0:T(1,128)} %bitcast.11, bf16[4,128,128]{2,1,0:T(8,128)(2,1)} %constant.8.refs_3_, bf16[2,8,128,128]{3,2,1,0:T(8,128)(2,1)} %refs_4_.1, bf16[2,8,128,128]{3,2,1,0:T(8,128)(2,1)} %refs_5_.1, ...), custom_call_target="tpu_custom_call" | custom-call | tf_op jit(solution)/shard_map/block/pallas_call | solution.py:754
  254.7 3.1 %copy.15 = bf16[1,8,128,1024]{3,2,1,0:T(8,128)(2,1)} copy(bf16[1,8,128,1024]{3,2,1,0:T(8,128)(2,1)} %bitcast.6) | data formatting | bytes 4194304

commit v2 on v1

--- a/solution.py
+++ b/solution.py
@@ -545,6 +545,11 @@
                 for piece in range(early // 2, early):
                     relay(2, piece, 0)
 
+        @pl.when((chunk == 3) & jnp.logical_not(inner))
+        def _():
+            for piece in range(early // 2):
+                relay(2, piece, 0)
+
         for offset in order:
             arrived(1, back_send, back_recv, chunk, offset).wait_recv()
         cut = pl.ds(pl.multiple_of(chunk * lanes, lanes), lanes)
@@ -605,14 +610,14 @@
             return when + stage * (pace + 1.5)
         if stage == 0:
             return pace * piece + (-3 if t == 2 else 32)
-        return pace * piece + (8 if t == 2 else 43)
+        return pace * piece + (3 if t == 2 else 39)
 
     def schedule(inside):
         places = {}
         for t in (2, 3):
             for piece in range(pieces):
                 for stage in range(2):
-                    if inside and t == 2 and stage == 0 and piece < early:
+                    if t == 2 and stage == 0 and piece < (early if inside else early // 2):
                         continue
                     when = expected(t, piece, stage, inside)
                     place = next((k for k, start in enumerate(starts[inside]) if start >= when - 2), 12)
@@ -691,37 +696,45 @@
             return_copy(block).start()
 
     for block in range(2):
+        swap_copy(block).wait_send()
+    gate_copy.wait_send()
+
+    @pl.loop(0, chunks)
+    def _(chunk):
+        for offset in order:
+            exchange(1, back_send, back_recv, chunk, offset).wait_send()
+
+    for piece in range(pieces):
+        own_copies(piece).wait_send()
+        for t in range(1, planes):
+            side_copy(expert_at[t], piece).wait_send()
+            for which in range(2):
+                core_copy(expert_at[t], piece, which).wait_send()
+
+    @pl.when(inner)
+    def _():
+        for piece in range(pieces):
+            far_own(piece).wait_send()
+            for t in range(1, planes):
+                forward(t, piece).wait_send()
+
+    def out_copy(block):
+        rows = pl.ds(block * step, step)
+        return pltpu.make_async_copy(acts.at[0, rows, :], out_ref.at[rows, :], local_sem.at[2 + block])
+
+    for block in range(2):
         return_copy(block).wait_recv()
         rows = pl.ds(block * step, step)
         for chunk in range(chunks):
             cut = slice(chunk * lanes, (chunk + 1) * lanes)
             final = resid[rows, cut].astype(jnp.float32) + total[0, rows, cut]
             final = final + spec_recv[chunk, rows, :].astype(jnp.float32)
-            out_ref[rows, cut] = final.astype(bf16)
+            acts[0, rows, cut] = final.astype(bf16)
+        out_copy(block).start()
 
     for block in range(2):
-        swap_copy(block).wait_send()
         return_copy(block).wait_send()
-    gate_copy.wait_send()
-
-    @pl.loop(0, chunks)
-    def _(chunk):
-        for offset in order:
-            exchange(1, back_send, back_recv, chunk, offset).wait_send()
-
-    for piece in range(pieces):
-        own_copies(piece).wait_send()
-        for t in range(1, planes):
-            side_copy(expert_at[t], piece).wait_send()
-            for which in range(2):
-                core_copy(expert_at[t], piece, which).wait_send()
-
-    @pl.when(inner)
-    def _():
-        for piece in range(pieces):
-            far_own(piece).wait_send()
-            for t in range(1, planes):
-                forward(t, piece).wait_send()
+        out_copy(block).wait()
 
 
 def per_device_fused(
@@ -754,7 +767,7 @@
     out = pl.pallas_call(
         lambda *refs: block_kernel(sizes, *refs),
         in_specs=[vmem] * 9 + [hbm] * 2,
-        out_specs=vmem,
+        out_specs=hbm,
         out_shape=jax.ShapeDtypeStruct((n_tokens, width), bf16),
         scratch_shapes=[
             pltpu.VMEM((n_tokens, n_tokens), bf16),
@@ -780,7 +793,7 @@
             dma((2, planes, pieces)),
             dma((5,)),
             dma((5,)),
-            dma((2,)),
+            dma((4,)),
         ],
         compiler_params=pltpu.CompilerParams(
             collective_id=0, has_side_effects=True, vmem_limit_bytes=67043328

time: 259 us -> 254 us (0.981)
  Pallas kernels: 251 us -> 247 us
    pallas_call x1, Pallas kernels: 251 us -> 247 us  [per_device_fused(): pl.pallas_call(lambda *refs: block_kernel(sizes, *refs), in_specs=[vmem]...]
where the time goes in v2:
time: 254 us; the launch traced here: 253 us
  Pallas kernels  247 us (97%)
  local copies, waits for them, and re-layouts  6.56 us (3%)
    pallas_call x1, Pallas kernels, per_device_fused(): pl.pallas_call(lambda *refs: block_kernel(sizes, *refs), in_specs=[vmem]...  247 us
    unnamed x3, local copies, waits for them, and re-layouts  6.56 us

profile of v2, /device:TPU:1, one launch (start us, length us, event | category | flops | bytes accessed | tf_op | source)
XLA Modules:
  0.0 253.3 jit_solution(15707989801393725295)
XLA Ops:
  0.0 1.7 copy.12
  1.7 1.7 copy.13
  3.5 246.7 %block.1 = bf16[1024,1024]{1,0:T(8,128)(2,1)} custom-call(bf16[1024,1024]{1,0:T(8,128)(2,1)} %bitcast.7, f32[1,1024]{1,0:T(1,128)} %bitcast.10, f32[1,1024]{1,0:T(1,128)} %bitcast.11, bf16[4,128,128]{2,1,0:T(8,128)(2,1)} %constant.8.refs_3_, bf16[2,8,128,128]{3,2,1,0:T(8,128)(2,1)} %refs_4_.1, bf16[2,8,128,128]{3,2,1,0:T(8,128)(2,1)} %refs_5_.1, ...), custom_call_target="tpu_custom_call" | custom-call | tf_op jit(solution)/shard_map/block/pallas_call | solution.py:767
  250.2 3.1 %copy.15 = bf16[1,8,128,1024]{3,2,1,0:T(8,128)(2,1)} copy(bf16[1,8,128,1024]{3,2,1,0:T(8,128)(2,1)} %bitcast.6) | data formatting | bytes 4194304

commit v3 on v2

--- a/solution.py
+++ b/solution.py
@@ -542,8 +542,11 @@
             def _():
                 for piece in range(PARTS, pieces):
                     forward(1, piece).start()
-                for piece in range(early // 2, early):
-                    relay(2, piece, 0)
+
+        @pl.when((chunk == 1) & inner)
+        def _():
+            for piece in range(early // 2, early):
+                relay(2, piece, 0)
 
         @pl.when((chunk == 3) & jnp.logical_not(inner))
         def _():

time: 254 us -> 254 us (level)
  no operation moved by 1% of the time
where the time goes in v3:
time: 254 us; the launch traced here: 253 us
  Pallas kernels  247 us (97%)
  local copies, waits for them, and re-layouts  6.56 us (3%)
    pallas_call x1, Pallas kernels, per_device_fused(): pl.pallas_call(lambda *refs: block_kernel(sizes, *refs), in_specs=[vmem]...  247 us
    unnamed x3, local copies, waits for them, and re-layouts  6.56 us

profile of v3, /device:TPU:1, one launch (start us, length us, event | category | flops | bytes accessed | tf_op | source)
XLA Modules:
  0.0 253.3 jit_solution(6559741422156170430)
XLA Ops:
  0.0 1.7 copy.12
  1.7 1.7 copy.13
  3.5 246.7 %block.1 = bf16[1024,1024]{1,0:T(8,128)(2,1)} custom-call(bf16[1024,1024]{1,0:T(8,128)(2,1)} %bitcast.7, f32[1,1024]{1,0:T(1,128)} %bitcast.10, f32[1,1024]{1,0:T(1,128)} %bitcast.11, bf16[4,128,128]{2,1,0:T(8,128)(2,1)} %constant.8.refs_3_, bf16[2,8,128,128]{3,2,1,0:T(8,128)(2,1)} %refs_4_.1, bf16[2,8,128,128]{3,2,1,0:T(8,128)(2,1)} %refs_5_.1, ...), custom_call_target="tpu_custom_call" | custom-call | tf_op jit(solution)/shard_map/block/pallas_call | solution.py:770
  250.2 3.1 %copy.15 = bf16[1,8,128,1024]{3,2,1,0:T(8,128)(2,1)} copy(bf16[1,8,128,1024]{3,2,1,0:T(8,128)(2,1)} %bitcast.6) | data formatting | bytes 4194304

commit v4 on v3

--- a/solution.py
+++ b/solution.py
@@ -131,7 +131,7 @@
 
 LANES = 256
 PARTS = 4
-EARLY_CHUNK = 3
+EARLY_CHUNK = 2
 
 
 def rank_tables(length, ranks):

time: 254 us -> 254 us (level)
  no operation moved by 1% of the time
where the time goes in v4:
time: 254 us; the launch traced here: 253 us
  Pallas kernels  247 us (97%)
  local copies, waits for them, and re-layouts  6.56 us (3%)
    pallas_call x1, Pallas kernels, per_device_fused(): pl.pallas_call(lambda *refs: block_kernel(sizes, *refs), in_specs=[vmem]...  247 us
    unnamed x3, local copies, waits for them, and re-layouts  6.56 us

profile of v4, /device:TPU:1, one launch (start us, length us, event | category | flops | bytes accessed | tf_op | source)
XLA Modules:
  0.0 253.3 jit_solution(9915463598769427754)
XLA Ops:
  0.0 1.7 copy.12
  1.7 1.7 copy.13
  3.5 246.7 %block.1 = bf16[1024,1024]{1,0:T(8,128)(2,1)} custom-call(bf16[1024,1024]{1,0:T(8,128)(2,1)} %bitcast.7, f32[1,1024]{1,0:T(1,128)} %bitcast.10, f32[1,1024]{1,0:T(1,128)} %bitcast.11, bf16[4,128,128]{2,1,0:T(8,128)(2,1)} %constant.8.refs_3_, bf16[2,8,128,128]{3,2,1,0:T(8,128)(2,1)} %refs_4_.1, bf16[2,8,128,128]{3,2,1,0:T(8,128)(2,1)} %refs_5_.1, ...), custom_call_target="tpu_custom_call" | custom-call | tf_op jit(solution)/shard_map/block/pallas_call | solution.py:770
  250.2 3.1 %copy.15 = bf16[1,8,128,1024]{3,2,1,0:T(8,128)(2,1)} copy(bf16[1,8,128,1024]{3,2,1,0:T(8,128)(2,1)} %bitcast.6) | data formatting | bytes 4194304
